TPU v7x, 512 devices: a whole 4x8x8 slice. The times are simulated.
512 devices in a mesh: grp: 8 (over y), dev: 64 (over z, x, core).
Axes of the slice: x: 4, y: 8, z: 8, core: 2. Of those that a mesh axis runs over, the one named last changes fastest.
Arguments:
- leaf_right: float32 [32, 131072], P(None, ('grp', 'dev')), may hold values from -6 to 6
- leaf_inverse: float32 [1024, 128, 128], P(('grp', 'dev')), may hold values from -1 to 2, as said below
- leaf_link: float32 [1024, 128, 128], P(('grp', 'dev')), may hold values from -0.25 to 0.25
- leaf_front: float32 [1024, 128, 128], P(('grp', 'dev')), may hold values from -0.1875 to 0.1875
- parents: int32 [1024], P(('grp', 'dev')), may hold values from 1 to 2, as said below
- front_rows: int32 [1024], P(('grp', 'dev')), may hold values from 0 to 15
- live_blocks: int32 [512], P(('grp', 'dev')), may hold values from 1 to 2, 896 in all
- front_right: float32 [32, 16384], P(None, ('grp', 'dev')), may hold values from -6 to 6
- front_inverse: float32 [16384, 2048], P(('grp', 'dev')), may hold values from -1 to 2, as said below
- front_couple: float32 [16384, 4096], P(('grp', 'dev')), may hold values from -0.046875 to 0.046875
- root_right: float32 [32, 2, 2048], P(None, None, 'dev'), may hold values from -6 to 6
- root_inverse: float32 [2, 2048, 2048], P(None, 'dev', 'grp'), may hold values from -1 to 2, as said below
- root_couple: float32 [1, 2048, 2048], P(None, 'dev', 'grp'), may hold values from -0.09375 to 0.09375
Outputs:
- leaf_solution: float32 [32, 131072], P(None, ('grp', 'dev'))
- front_solution: float32 [32, 16384], P(None, 'grp')
- root_solution: float32 [32, 2, 2048], P(None, None, 'dev')
Inputs may be any that keep to these rules, and one draw needn't show every extreme that they name: For local block k = b mod 2, parents[b] lies in k + 1 .. 2; the value 2 means no parent among the piece's blocks. A piece's live blocks are its first live_blocks[p]; some piece has all 2. `leaf_inverse`: each block is lower triangular with a positive diagonal. `front_inverse`: each front's block is lower triangular with a positive diagonal. `root_inverse`: each level's block is lower triangular with a positive diagonal.
All inputs are finite; a program needn't handle non-finite values.
Results may differ from a plain program's by a relative error of at most 0.0003.
Values sent between devices are 32-bit elements; how exact they have to be, the bound alone decides.
No kernel may reach another device: no remote copies, remote signals or barrier semaphores. Data moves between devices by JAX's collectives and lax.ppermute only.
A program may use at most 64 MiB of HBM per device.

v0:
```python
import jax
import jax.numpy as jnp
from jax import lax
from jax.sharding import Mesh
from jax.sharding import PartitionSpec as P

EXACT = lax.Precision.HIGH
NEAR = ("x", "core")
DEV = ("z", "x", "core")


def mm(left, right):
    return jnp.dot(left, right, precision=EXACT)


def mmt(left, right):
    return jnp.einsum("rn,mn->rm", left, right, precision=EXACT)


def swap(chunks, axes):
    return lax.all_to_all(chunks, axes, 0, 0, tiled=True)


def spread(values, axes, count):
    return swap(jnp.broadcast_to(values[None], (count,) + values.shape), axes)


def reduce_over(values, axes, count):
    return jnp.sum(spread(values, axes, count), 0)


def make_body(sizes):
    n_grp, n_z = (sizes["grp"], sizes["z"])
    n_near = sizes["x"] * sizes["core"]
    n_dev = n_z * n_near

    def body(
        leaf_right,
        leaf_inverse,
        leaf_link,
        leaf_front,
        parents,
        front_rows,
        live_blocks,
        front_right,
        front_inverse,
        front_couple,
        root_right,
        root_inverse,
        root_couple,
    ):
        rows = leaf_right.shape[0]
        width = leaf_inverse.shape[1]
        front_order = front_inverse.shape[1]
        n_front = front_order // width
        share = front_inverse.shape[0]
        slab = share * n_z
        part = root_inverse.shape[2]
        live = live_blocks[0]
        my_z = lax.axis_index("z")

        def near_sum(natural):
            chunks = natural.reshape(rows, n_z, n_near, share).transpose(2, 0, 1, 3)
            return jnp.sum(swap(chunks.reshape(n_near, rows, slab), NEAR), 0)

        def own(values):
            return lax.dynamic_slice_in_dim(values, my_z * share, share, 1)

        blocks = front_inverse.reshape(share, n_z, part).transpose(1, 0, 2)
        wide = jnp.concatenate([blocks, root_inverse, root_couple], 0)
        wide = lax.all_gather(wide, "z", axis=1, tiled=True)
        front_slab, w_low, w_high, link = (wide[:n_z], wide[n_z], wide[n_z + 1], wide[n_z + 2])
        has_parent = parents[0] < live
        right0, right1 = (leaf_right[:, :width], leaf_right[:, width:])
        solved0 = jnp.where(live > 0, mm(right0, leaf_inverse[0]), 0.0)
        lifted = jnp.where(has_parent, mm(solved0, leaf_link[0]), 0.0)
        solved1 = jnp.where(live > 1, mm(right1 - lifted, leaf_inverse[1]), 0.0)
        given0, given1 = (mm(solved0, leaf_front[0]), mm(solved1, leaf_front[1]))
        slots = jnp.arange(n_front, dtype=jnp.int32)[None, :, None]
        placed = jnp.where(slots == front_rows[0], given0[:, None, :], 0.0) + jnp.where(
            slots == front_rows[1], given1[:, None, :], 0.0
        )
        update = near_sum(placed.reshape(rows, front_order))
        here = (jnp.arange(slab, dtype=jnp.int32) // share == my_z)[None, :]
        start = jnp.where(here, jnp.tile(front_right, (1, n_z)), 0.0) - update
        start = jnp.broadcast_to(reduce_over(start, "z", n_z)[None], (n_z, rows, slab))
        terms = jnp.einsum("zrk,zkn->zrn", start, front_slab, precision=EXACT)
        terms = lax.optimization_barrier(terms).reshape(n_z, rows, n_near, share)
        terms = terms.transpose(2, 1, 0, 3).reshape(n_near, rows, slab)
        y_slab = jnp.sum(swap(terms, NEAR), 0)
        y_own = own(y_slab)
        raised = mm(y_own, front_couple)
        half = rows // 2
        chunks = raised.reshape(2, half, 2, n_dev, share).transpose(3, 1, 0, 2, 4)
        raised = jnp.sum(swap(chunks.reshape(n_dev, half, 4 * share), DEV), 0)
        given = root_right.reshape(2, half, 2, share).transpose(1, 0, 2, 3).reshape(half, 4 * share)
        given = jnp.where(lax.axis_index("grp") == 0, given, 0.0) - raised
        given = jnp.sum(
            spread(given, ("grp", "z"), n_grp * n_z).reshape(n_grp, n_z, half, 4 * share), 0
        )
        given = (
            given.reshape(n_z, half, 2, 2, share).transpose(3, 2, 1, 0, 4).reshape(2, rows, slab)
        )
        low, high = (given[0], given[1])
        y_high = reduce_over(mm(high, w_high), NEAR, n_near)
        low = low - reduce_over(mmt(y_high, link), "grp", n_grp)
        y_low = reduce_over(mm(low, w_low), NEAR, n_near)
        x_low = reduce_over(mmt(y_low, w_low), "grp", n_grp)
        y_high = y_high - reduce_over(mm(x_low, link), NEAR, n_near)
        x_high = reduce_over(mmt(y_high, w_high), "grp", n_grp)
        both = jnp.concatenate([x_low, x_high], 1)
        whole = spread(both, NEAR, n_near).reshape(n_near, rows, 2, n_z, share)
        whole = whole.transpose(1, 2, 3, 0, 4).reshape(rows, 2 * front_order)
        rest = y_own - mmt(whole, front_couple)
        rest = rest.reshape(4, rows // 4, share).transpose(1, 0, 2).reshape(rows // 4, 4 * share)
        rest = spread(rest, DEV, n_dev).reshape(n_dev, rows // 4, 4, share)
        rest = rest.reshape(n_z, n_near, rows // 4, 4, share)
        rest = rest.transpose(0, 3, 2, 1, 4).reshape(n_z, rows, part)
        solved = jnp.einsum("zrn,zkn->zrk", rest, front_slab, precision=EXACT)
        front_solution = spread(jnp.sum(solved, 0), NEAR, n_near)
        front_solution = front_solution.reshape(n_near, rows, n_z, share)
        front_solution = front_solution.transpose(1, 2, 0, 3).reshape(rows, front_order)

        def back(solved, block):
            picked = lax.dynamic_slice(
                front_solution, (0, front_rows[block] * width), (rows, width)
            )
            return solved - mmt(picked, leaf_front[block])

        base0, base1 = (back(solved0, 0), back(solved1, 1))
        leaf1 = jnp.where(live > 1, mmt(base1, leaf_inverse[1]), 0.0)
        carried = jnp.where(has_parent, mmt(leaf1, leaf_link[0]), 0.0)
        leaf0 = jnp.where(live > 0, mmt(base0 - carried, leaf_inverse[0]), 0.0)
        leaf_solution = jnp.concatenate([leaf0, leaf1], 1)
        return (leaf_solution, front_solution, jnp.stack([own(x_low), own(x_high)], 1))

    return body


def solution(mesh):
    n_grp, n_dev = (mesh.shape["grp"], mesh.shape["dev"])
    fine = Mesh(mesh.devices.reshape(n_grp, n_dev // 8, 4, 2), ("grp", "z", "x", "core"))
    every = ("grp",) + DEV
    in_specs = (
        P(None, every),
        P(every, None, None),
        P(every, None, None),
        P(every, None, None),
        P(every),
        P(every),
        P(every),
        P(None, every),
        P(every, None),
        P(every, None),
        P(None, None, DEV),
        P(None, DEV, "grp"),
        P(None, DEV, "grp"),
    )
    out_specs = (P(None, every), P(None, "grp"), P(None, None, DEV))
    body = make_body(dict(fine.shape))
    return jax.shard_map(body, mesh=fine, in_specs=in_specs, out_specs=out_specs, check_vma=False)
```

profile of v0, /device:TPU:1, one launch (start us, length us, event | category | flops | bytes accessed | tf_op | source)
XLA Modules:
  0.0 311.3 jit_solution(14920914953933961020)
XLA Ops:
  7.2 1.0 copy.88
  8.3 1.6 pad_maximum_fusion
  11.2 1.4 fusion.51
  14.2 1.0 convolution_select_fusion.5
  15.2 1.0 fusion.9
  16.2 1.0 convolution_select_fusion.3
  17.2 1.0 fusion.18
  19.5 1.0 reshape.150
  20.5 10.2 %all-to-all-start = ((f32[8,32,256]{2,1,0:T(8,128)}), f32[8,32,256]{2,1,0:T(8,128)S(1)}, u32[]{:S(2)}, u32[]{:S(2)}) async-start(f32[8,32,256]{2,1,0:T(8,128)} %reshape.150), calls=%async_computation | async-start | bytes 524288 | tf_op jit(solution)/shard_map/all_to_all | solution.py:21
  30.7 6.4 %all-to-all-done = f32[8,32,256]{2,1,0:T(8,128)S(1)} async-done(((f32[8,32,256]{2,1,0:T(8,128)}), f32[8,32,256]{2,1,0:T(8,128)S(1)}, u32[]{:S(2)}, u32[]{:S(2)}) %all-to-all-start) | async-done | bytes 262176 | tf_op jit(solution)/shard_map/all_to_all | solution.py:21
  37.2 20.2 %all_to_all.70 = f32[8,32,256]{2,1,0:T(8,128)S(1)} all-to-all(f32[8,32,256]{2,1,0:T(8,128)S(1)} %broadcast_in_dim.159), channel_id=1, replica_groups=mesh['grp'=8,'z'=8,'x'=4,'core'=2] {'z'}, dimensions={0} | all-to-all | bytes 524288 | tf_op jit(solution)/shard_map/all_to_all | solution.py:21
  57.5 8.6 %all-gather.2.cloned.1.call-done = f32[11,256,256]{2,1,0:T(8,128)} async-done(((f32[11,32,256]{2,1,0:T(8,128)}), f32[11,256,256]{2,1,0:T(8,128)}) %all-gather.2.cloned.1.call-update) | async-done | bytes 2883600 | tf_op jit(solution)/shard_map/all_gather | solution.py:71
  66.1 2.3 fusion.2
  69.3 1.0 reshape.153
  70.3 6.6 %all-to-all-start.2 = ((f32[8,32,256]{2,1,0:T(8,128)}), f32[8,32,256]{2,1,0:T(8,128)S(1)}, u32[]{:S(2)}, u32[]{:S(2)}) async-start(f32[8,32,256]{2,1,0:T(8,128)} %reshape.153), calls=%async_computation.2 | async-start | bytes 524288 | tf_op jit(solution)/shard_map/all_to_all | solution.py:21
  76.9 6.5 %all-to-all-done.2 = f32[8,32,256]{2,1,0:T(8,128)S(1)} async-done(((f32[8,32,256]{2,1,0:T(8,128)}), f32[8,32,256]{2,1,0:T(8,128)S(1)}, u32[]{:S(2)}, u32[]{:S(2)}) %all-to-all-start.2) | async-done | bytes 262176 | tf_op jit(solution)/shard_map/all_to_all | solution.py:21
  84.6 1.6 copy.74
  86.1 2.4 copy.75
  88.5 6.7 %all-to-all-start.3 = ((f32[64,16,128]{2,1,0:T(8,128)}), f32[64,16,128]{2,1,0:T(8,128)}, u32[]{:S(2)}, u32[]{:S(2)}) async-start(f32[64,16,128]{2,1,0:T(8,128)} %copy.75), calls=%async_computation.3 | async-start | bytes 1048576 | tf_op jit(solution)/shard_map/all_to_all | solution.py:21
  95.3 17.5 %all-to-all-done.3 = f32[64,16,128]{2,1,0:T(8,128)} async-done(((f32[64,16,128]{2,1,0:T(8,128)}), f32[64,16,128]{2,1,0:T(8,128)}, u32[]{:S(2)}, u32[]{:S(2)}) %all-to-all-start.3) | async-done | bytes 524320 | tf_op jit(solution)/shard_map/all_to_all | solution.py:21
  112.8 1.1 reduce_sum.108
  114.0 25.6 %all_to_all.71 = f32[64,16,128]{2,1,0:T(8,128)} all-to-all(f32[64,16,128]{2,1,0:T(8,128)S(1)} %broadcast_in_dim.162), channel_id=1, replica_groups=mesh['grp'=8,'z'=8,'x'=4,'core'=2] {'grp','z'}, dimensions={0} | all-to-all | bytes 1048576 | tf_op jit(solution)/shard_map/all_to_all | solution.py:21
  139.5 1.1 reduce_sum.109
  141.6 1.1 copy.89
  145.1 13.3 %all_to_all.72 = f32[8,32,256]{2,1,0:T(8,128)} all-to-all(f32[8,32,256]{2,1,0:T(8,128)S(1)} %broadcast_in_dim.163), channel_id=1, replica_groups=mesh['grp'=8,'z'=8,'x'=4,'core'=2] {'x','core'}, dimensions={0} | all-to-all | bytes 524288 | tf_op jit(solution)/shard_map/all_to_all | solution.py:21
  158.4 1.0 reduce_sum.110
  159.7 13.9 %all_to_all.73 = f32[8,32,256]{2,1,0:T(8,128)} all-to-all(f32[8,32,256]{2,1,0:T(8,128)S(1)} %broadcast_in_dim.164), channel_id=1, replica_groups=mesh['grp'=8,'z'=8,'x'=4,'core'=2] {'grp'}, dimensions={0} | all-to-all | bytes 524288 | tf_op jit(solution)/shard_map/all_to_all | solution.py:21
  173.6 1.6 reduce_sum.111
  176.0 1.6 slice_subtract_fusion
  177.6 1.0 sub.49
  178.8 12.2 %all_to_all.74 = f32[8,32,256]{2,1,0:T(8,128)} all-to-all(f32[8,32,256]{2,1,0:T(8,128)S(1)} %broadcast_in_dim.165), channel_id=1, replica_groups=mesh['grp'=8,'z'=8,'x'=4,'core'=2] {'x','core'}, dimensions={0} | all-to-all | bytes 524288 | tf_op jit(solution)/shard_map/all_to_all | solution.py:21
  191.0 1.0 reduce_sum.113
  192.3 13.4 %all_to_all.75 = f32[8,32,256]{2,1,0:T(8,128)} all-to-all(f32[8,32,256]{2,1,0:T(8,128)S(1)} %broadcast_in_dim.166), channel_id=1, replica_groups=mesh['grp'=8,'z'=8,'x'=4,'core'=2] {'grp'}, dimensions={0} | all-to-all | bytes 524288 | tf_op jit(solution)/shard_map/all_to_all | solution.py:21
  206.8 12.0 %all_to_all.76 = f32[8,32,256]{2,1,0:T(8,128)} all-to-all(f32[8,32,256]{2,1,0:T(8,128)S(1)} %broadcast_in_dim.167), channel_id=1, replica_groups=mesh['grp'=8,'z'=8,'x'=4,'core'=2] {'x','core'}, dimensions={0} | all-to-all | bytes 524288 | tf_op jit(solution)/shard_map/all_to_all | solution.py:21
  220.2 13.4 %all_to_all.77 = f32[8,32,256]{2,1,0:T(8,128)} all-to-all(f32[8,32,256]{2,1,0:T(8,128)S(1)} %broadcast_in_dim.168), channel_id=1, replica_groups=mesh['grp'=8,'z'=8,'x'=4,'core'=2] {'grp'}, dimensions={0} | all-to-all | bytes 524288 | tf_op jit(solution)/shard_map/all_to_all | solution.py:21
  234.6 14.9 %all_to_all.78 = f32[8,32,512]{2,1,0:T(8,128)} all-to-all(f32[8,32,512]{2,1,0:T(8,128)S(1)} %broadcast_in_dim.169), channel_id=1, replica_groups=mesh['grp'=8,'z'=8,'x'=4,'core'=2] {'x','core'}, dimensions={0} | all-to-all | bytes 1048576 | tf_op jit(solution)/shard_map/all_to_all | solution.py:21
  249.5 2.8 reshape.158
  252.3 4.1 %copy.77 = f32[32,2,8,8,32]{4,3,2,1,0:T(8,128)} copy(f32[32,2,8,8,32]{4,2,1,0,3:T(8,128)} %bitcast.110) | data formatting | bytes 1048576 | tf_op jit(solution)/shard_map/transpose | solution.py:113
  256.4 3.3 %reshape.159 = f32[32,4096]{1,0:T(8,128)} reshape(f32[32,2,8,8,32]{4,3,2,1,0:T(8,128)} %copy.77) | data formatting | bytes 1048576 | tf_op jit(solution)/shard_map/reshape | solution.py:113
  259.8 1.4 fusion.8
  262.0 5.9 %all-to-all-start.12 = ((f32[64,8,128]{2,1,0:T(8,128)}), f32[64,8,128]{2,1,0:T(8,128)}, u32[]{:S(2)}, u32[]{:S(2)}) async-start(f32[64,8,128]{2,1,0:T(8,128)} %broadcast_in_dim.171), calls=%async_computation.12 | async-start | bytes 524288 | tf_op jit(solution)/shard_map/all_to_all | solution.py:21
  269.3 11.7 %all-to-all-done.12 = f32[64,8,128]{2,1,0:T(8,128)} async-done(((f32[64,8,128]{2,1,0:T(8,128)}), f32[64,8,128]{2,1,0:T(8,128)}, u32[]{:S(2)}, u32[]{:S(2)}) %all-to-all-start.12) | async-done | bytes 262176 | tf_op jit(solution)/shard_map/all_to_all | solution.py:21
  281.0 2.4 reshape_reshape.4
  283.3 2.9 copy.79
  286.2 2.2 reshape.161
  288.4 2.0 fusion.4
  291.2 3.8 %all-to-all-start.13 = ((f32[8,32,256]{2,1,0:T(8,128)}), f32[8,32,256]{2,1,0:T(8,128)S(1)}, u32[]{:S(2)}, u32[]{:S(2)}) async-start(f32[8,32,256]{2,1,0:T(8,128)} %broadcast_in_dim.172), calls=%async_computation.13 | async-start | bytes 524288 | tf_op jit(solution)/shard_map/all_to_all | solution.py:21
  295.8 5.7 %all-to-all-done.13 = f32[8,32,256]{2,1,0:T(8,128)S(1)} async-done(((f32[8,32,256]{2,1,0:T(8,128)}), f32[8,32,256]{2,1,0:T(8,128)S(1)}, u32[]{:S(2)}, u32[]{:S(2)}) %all-to-all-start.13) | async-done | bytes 262176 | tf_op jit(solution)/shard_map/all_to_all | solution.py:21
  (101 shorter events, 18.9 us)
Async XLA Ops:
  7.2 76.2 %copy-start = (f32[32,4096]{1,0:T(8,128)S(1)}, f32[32,4096]{1,0:T(8,128)}, u32[]{:S(2)}) copy-start(f32[32,4096]{1,0:T(8,128)} %param.22) | copy-start | bytes 1572868
  7.2 11.3 %copy-start.3 = (f32[2,128,128]{2,1,0:T(8,128)S(1)}, f32[2,128,128]{2,1,0:T(8,128)}, u32[]{:S(2)}) copy-start(f32[2,128,128]{2,1,0:T(8,128)} %param.16) | copy-start | bytes 393220
  7.2 59.0 %all-gather.2.cloned.1.call-start = ((), (), s32[]{:S(2)}) async-start(), calls=%async_computation.14 | async-start | bytes 3244032 | tf_op jit(solution)/shard_map/all_gather | solution.py:71
  17.2 1.0 copy-start.9
  19.0 11.6 %copy-start.15 = (f32[32,32]{1,0:T(8,128)S(1)}, f32[32,32]{1,0:T(8,128)}, u32[]{:S(2)}) copy-start(f32[32,32]{1,0:T(8,128)} %param.20) | copy-start | bytes 12292
  20.5 16.7 %all-to-all-start = ((f32[8,32,256]{2,1,0:T(8,128)}), f32[8,32,256]{2,1,0:T(8,128)S(1)}, u32[]{:S(2)}, u32[]{:S(2)}) async-start(f32[8,32,256]{2,1,0:T(8,128)} %reshape.150), calls=%async_computation | async-start | bytes 524288 | tf_op jit(solution)/shard_map/all_to_all | solution.py:21
  70.3 13.1 %all-to-all-start.2 = ((f32[8,32,256]{2,1,0:T(8,128)}), f32[8,32,256]{2,1,0:T(8,128)S(1)}, u32[]{:S(2)}, u32[]{:S(2)}) async-start(f32[8,32,256]{2,1,0:T(8,128)} %reshape.153), calls=%async_computation.2 | async-start | bytes 524288 | tf_op jit(solution)/shard_map/all_to_all | solution.py:21
  83.4 2.7 copy-start.11
  84.5 10.7 %copy-start.14 = (f32[32,2,32]{2,1,0:T(2,128)S(1)}, f32[32,2,32]{2,1,0:T(2,128)}, u32[]{:S(2)}) copy-start(f32[32,2,32]{2,1,0:T(2,128)} %param.23) | copy-start | bytes 24580
  88.5 55.6 %copy-start.1 = (f32[11,256,256]{2,1,0:T(8,128)S(1)}, f32[11,256,256]{2,1,0:T(8,128)}, u32[]{:S(2)}) copy-start(f32[11,256,256]{2,1,0:T(8,128)} %all-gather.2.cloned.1.call-done) | copy-start | bytes 8650756
  88.5 24.3 %all-to-all-start.3 = ((f32[64,16,128]{2,1,0:T(8,128)}), f32[64,16,128]{2,1,0:T(8,128)}, u32[]{:S(2)}, u32[]{:S(2)}) async-start(f32[64,16,128]{2,1,0:T(8,128)} %copy.75), calls=%async_computation.3 | async-start | bytes 1048576 | tf_op jit(solution)/shard_map/all_to_all | solution.py:21
  142.7 0.7 copy-start.2
  159.4 14.2 %copy-start.7 = (f32[32,256]{1,0:T(8,128)}, f32[32,256]{1,0:T(8,128)S(1)}, u32[]{:S(2)}) copy-start(f32[32,256]{1,0:T(8,128)S(1)} %reduce_sum.110) | copy-start | bytes 98308
  177.6 42.3 %copy-start.8 = (f32[32,256]{1,0:T(8,128)S(1)}, f32[32,256]{1,0:T(8,128)}, u32[]{:S(2)}) copy-start(f32[32,256]{1,0:T(8,128)} %copy-done.7) | copy-start | bytes 98308
  252.3 7.4 %copy-start.12 = (f32[32,256]{1,0:T(8,128)S(1)}, f32[32,256]{1,0:T(8,128)}, u32[]{:S(2)}) copy-start(f32[32,256]{1,0:T(8,128)} %copy-done.11) | copy-start | bytes 98308
  262.0 19.0 %all-to-all-start.12 = ((f32[64,8,128]{2,1,0:T(8,128)}), f32[64,8,128]{2,1,0:T(8,128)}, u32[]{:S(2)}, u32[]{:S(2)}) async-start(f32[64,8,128]{2,1,0:T(8,128)} %broadcast_in_dim.171), calls=%async_computation.12 | async-start | bytes 524288 | tf_op jit(solution)/shard_map/all_to_all | solution.py:21
  290.4 12.4 %copy-start.4 = (f32[2,128,128]{2,1,0:T(8,128)S(1)}, f32[2,128,128]{2,1,0:T(8,128)}, u32[]{:S(2)}) copy-start(f32[2,128,128]{2,1,0:T(8,128)} %param.16) | copy-start | bytes 393220
  290.4 12.4 %copy-start.10 = (f32[32,128]{1,0:T(8,128)S(1)}, f32[32,128]{1,0:T(8,128)}, u32[]{:S(2)}) copy-start(f32[32,128]{1,0:T(8,128)} %copy-done.9) | copy-start | bytes 49156
  290.5 12.6 %copy-start.5 = (f32[2,128,128]{2,1,0:T(8,128)S(1)}, f32[2,128,128]{2,1,0:T(8,128)}, u32[]{:S(2)}) copy-start(f32[2,128,128]{2,1,0:T(8,128)} %param.14) | copy-start | bytes 393220
  291.2 12.2 %copy-start.13 = (f32[2,128,128]{2,1,0:T(8,128)S(1)}, f32[2,128,128]{2,1,0:T(8,128)}, u32[]{:S(2)}) copy-start(f32[2,128,128]{2,1,0:T(8,128)} %param.15) | copy-start | bytes 393220
  291.2 10.2 %all-to-all-start.13 = ((f32[8,32,256]{2,1,0:T(8,128)}), f32[8,32,256]{2,1,0:T(8,128)S(1)}, u32[]{:S(2)}, u32[]{:S(2)}) async-start(f32[8,32,256]{2,1,0:T(8,128)} %broadcast_in_dim.172), calls=%async_computation.13 | async-start | bytes 524288 | tf_op jit(solution)/shard_map/all_to_all | solution.py:21
  302.8 1.6 copy-start.6
Sparse Core Ops, SparseCore 0:
  10.1 56.0 all-gather.1
where the time goes:
time: 313 us; the launch traced here: 311 us
  blocking collectives  139 us (44%)
  waiting for transfers between devices  56.3 us (18%)
  local copies, waits for them, and re-layouts  37.6 us (12%)
  starting transfers between devices  33.2 us (11%)
  between operations  17.3 us (6%)
  other arithmetic  14.9 us (5%)
  matrix products  13 us (4%)
    all_to_all x9, blocking collectives, swap(): return lax.all_to_all(chunks, axes, 0, 0, tiled=True)  139 us
    all_to_all x5, waiting for transfers between devices, swap(): return lax.all_to_all(chunks, axes, 0, 0, tiled=True)  47.7 us
    all_to_all x5, starting transfers between devices, swap(): return lax.all_to_all(chunks, axes, 0, 0, tiled=True)  33.1 us
    all_gather x1, waiting for transfers between devices, body(): wide = lax.all_gather(wide, 'z', axis=1, tiled=True)  8.64 us
    reduce_sum x7, other arithmetic, reduce_over(): return jnp.sum(spread(values, axes, count), 0)  6.46 us
  transfers between devices with their start and end apart: 6, of which 6 were waited for; matrix products, arithmetic and copies ran while one was open for 3% of the time, Pallas kernels for 0%

commit v1 on v0

--- a/solution.py
+++ b/solution.py
@@ -68,7 +68,9 @@
 
         blocks = front_inverse.reshape(share, n_z, part).transpose(1, 0, 2)
         wide = jnp.concatenate([blocks, root_inverse, root_couple], 0)
-        wide = lax.all_gather(wide, "z", axis=1, tiled=True)
+        wide = jnp.concatenate(
+            lax.all_to_all(jnp.stack([wide] * lax.axis_size("z")), "z", 0, 0), axis=1
+        )
         front_slab, w_low, w_high, link = (wide[:n_z], wide[n_z], wide[n_z + 1], wide[n_z + 2])
         has_parent = parents[0] < live
         right0, right1 = (leaf_right[:, :width], leaf_right[:, width:])

time: 313 us -> 355 us (1.13)
  waiting for transfers between devices: 56.3 us -> 138 us
  blocking collectives: 139 us -> 91.2 us
  starting transfers between devices: 33.2 us -> 52.3 us
  between operations: 17.3 us -> 3.84 us
  local copies, waits for them, and re-layouts: 37.6 us -> 47 us
  other arithmetic: 14.9 us -> 10.2 us
    all_to_all x0 -> x1, waiting for transfers between devices: none -> 64.8 us  [body(): lax.all_to_all(jnp.stack([wide] * lax.axis_size('z')), 'z', 0, 0)]
    all_to_all x9 -> x7, blocking collectives: 139 us -> 91.2 us  [swap(): return lax.all_to_all(chunks, axes, 0, 0, tiled=True)]
    all_to_all x5 -> x7, waiting for transfers between devices: 47.7 us -> 73.2 us  [swap(): return lax.all_to_all(chunks, axes, 0, 0, tiled=True)]
    all_to_all x5 -> x7, starting transfers between devices: 33.1 us -> 47.9 us  [swap(): return lax.all_to_all(chunks, axes, 0, 0, tiled=True)]
    all_gather x1 -> x0, waiting for transfers between devices: 8.64 us -> none  [body(): wide = lax.all_gather(wide, 'z', axis=1, tiled=True)]
    all_to_all x0 -> x1, starting transfers between devices: none -> 4.41 us  [body(): lax.all_to_all(jnp.stack([wide] * lax.axis_size('z')), 'z', 0, 0)]
  transfers between devices with their start and end apart: 6 -> 8, of which waited for: 6 -> 8; matrix products, arithmetic and copies ran while one was open for 3% -> 1% of each run, Pallas kernels for 0% -> 0%
where the time goes in v1:
time: 355 us; the launch traced here: 353 us
  waiting for transfers between devices  138 us (39%)
  blocking collectives  91.2 us (26%)
  starting transfers between devices  52.3 us (15%)
  local copies, waits for them, and re-layouts  47 us (13%)
  matrix products  10.3 us (3%)
  other arithmetic  10.2 us (3%)
  between operations  3.84 us (1%)
    all_to_all x7, blocking collectives, swap(): return lax.all_to_all(chunks, axes, 0, 0, tiled=True)  91.2 us
    all_to_all x7, waiting for transfers between devices, swap(): return lax.all_to_all(chunks, axes, 0, 0, tiled=True)  73.2 us
    all_to_all x1, waiting for transfers between devices, body(): lax.all_to_all(jnp.stack([wide] * lax.axis_size('z')), 'z', 0, 0)  64.8 us
    all_to_all x7, starting transfers between devices, swap(): return lax.all_to_all(chunks, axes, 0, 0, tiled=True)  47.9 us
  transfers between devices with their start and end apart: 8, of which 8 were waited for; matrix products, arithmetic and copies ran while one was open for 1% of the time, Pallas kernels for 0%

profile of v1, /device:TPU:1, one launch (start us, length us, event | category | flops | bytes accessed | tf_op | source)
XLA Modules:
  0.0 352.8 jit_solution(8247963099260739278)
XLA Ops:
  2.0 1.3 fusion.41
  4.7 1.0 convolution_select_fusion.5
  6.6 1.0 fusion.2
  10.8 1.0 reshape.163
  11.8 10.2 %all-to-all-start = ((f32[8,32,256]{2,1,0:T(8,128)}), f32[8,32,256]{2,1,0:T(8,128)S(1)}, u32[]{:S(2)}, u32[]{:S(2)}) async-start(f32[8,32,256]{2,1,0:T(8,128)} %reshape.163), calls=%async_computation | async-start | bytes 524288 | tf_op jit(solution)/shard_map/all_to_all | solution.py:21
  22.1 6.4 %all-to-all-done = f32[8,32,256]{2,1,0:T(8,128)S(1)} async-done(((f32[8,32,256]{2,1,0:T(8,128)}), f32[8,32,256]{2,1,0:T(8,128)S(1)}, u32[]{:S(2)}, u32[]{:S(2)}) %all-to-all-start) | async-done | bytes 262176 | tf_op jit(solution)/shard_map/all_to_all | solution.py:21
  29.2 5.6 %all-to-all-start.1 = ((f32[8,32,256]{2,1,0:T(8,128)}), f32[8,32,256]{2,1,0:T(8,128)S(1)}, u32[]{:S(2)}, u32[]{:S(2)}) async-start(f32[8,32,256]{2,1,0:T(8,128)} %broadcast_in_dim.159), calls=%async_computation.1 | async-start | bytes 524288 | tf_op jit(solution)/shard_map/all_to_all | solution.py:21
  34.9 10.1 %all-to-all-done.1 = f32[8,32,256]{2,1,0:T(8,128)S(1)} async-done(((f32[8,32,256]{2,1,0:T(8,128)}), f32[8,32,256]{2,1,0:T(8,128)S(1)}, u32[]{:S(2)}, u32[]{:S(2)}) %all-to-all-start.1) | async-done | bytes 262176 | tf_op jit(solution)/shard_map/all_to_all | solution.py:21
  45.0 2.0 stack.8
  47.0 4.4 %all-to-all-start.2 = ((f32[8,11,32,256]{3,2,1,0:T(8,128)}), f32[8,11,32,256]{3,2,1,0:T(8,128)}, u32[]{:S(2)}, u32[]{:S(2)}) async-start(f32[8,11,32,256]{3,2,1,0:T(8,128)} %stack.8), calls=%async_computation.2 | async-start | bytes 5767168 | tf_op jit(solution)/shard_map/all_to_all | solution.py:72
  51.5 64.8 %all-to-all-done.2 = f32[8,11,32,256]{3,2,1,0:T(8,128)} async-done(((f32[8,11,32,256]{3,2,1,0:T(8,128)}), f32[8,11,32,256]{3,2,1,0:T(8,128)}, u32[]{:S(2)}, u32[]{:S(2)}) %all-to-all-start.2) | async-done | bytes 2883616 | tf_op jit(solution)/shard_map/all_to_all | solution.py:72
  116.3 1.7 slice.80
  118.8 1.2 reshape.166
  120.1 2.8 copy.97
  122.9 2.2 reshape.167
  125.1 7.5 %all-to-all-start.3 = ((f32[8,32,256]{2,1,0:T(8,128)}), f32[8,32,256]{2,1,0:T(8,128)S(1)}, u32[]{:S(2)}, u32[]{:S(2)}) async-start(f32[8,32,256]{2,1,0:T(8,128)} %reshape.167), calls=%async_computation.3 | async-start | bytes 524288 | tf_op jit(solution)/shard_map/all_to_all | solution.py:21
  132.7 6.5 %all-to-all-done.3 = f32[8,32,256]{2,1,0:T(8,128)S(1)} async-done(((f32[8,32,256]{2,1,0:T(8,128)}), f32[8,32,256]{2,1,0:T(8,128)S(1)}, u32[]{:S(2)}, u32[]{:S(2)}) %all-to-all-start.3) | async-done | bytes 262176 | tf_op jit(solution)/shard_map/all_to_all | solution.py:21
  139.6 2.0 reshape.168
  141.7 3.2 copy.84
  144.8 2.4 copy.85
  147.2 5.1 %all-to-all-start.4 = ((f32[64,16,128]{2,1,0:T(8,128)}), f32[64,16,128]{2,1,0:T(8,128)S(1)}, u32[]{:S(2)}, u32[]{:S(2)}) async-start(f32[64,16,128]{2,1,0:T(8,128)} %copy.85), calls=%async_computation.4 | async-start | bytes 1048576 | tf_op jit(solution)/shard_map/all_to_all | solution.py:21
  152.5 17.6 %all-to-all-done.4 = f32[64,16,128]{2,1,0:T(8,128)S(1)} async-done(((f32[64,16,128]{2,1,0:T(8,128)}), f32[64,16,128]{2,1,0:T(8,128)S(1)}, u32[]{:S(2)}, u32[]{:S(2)}) %all-to-all-start.4) | async-done | bytes 524320 | tf_op jit(solution)/shard_map/all_to_all | solution.py:21
  171.1 10.0 %all-to-all-start.5 = ((f32[64,16,128]{2,1,0:T(8,128)}), f32[64,16,128]{2,1,0:T(8,128)}, u32[]{:S(2)}, u32[]{:S(2)}) async-start(f32[64,16,128]{2,1,0:T(8,128)} %broadcast_in_dim.162), calls=%async_computation.5 | async-start | bytes 1048576 | tf_op jit(solution)/shard_map/all_to_all | solution.py:21
  181.1 1.2 fusion.40
  182.3 15.1 %all-to-all-done.5 = f32[64,16,128]{2,1,0:T(8,128)} async-done(((f32[64,16,128]{2,1,0:T(8,128)}), f32[64,16,128]{2,1,0:T(8,128)}, u32[]{:S(2)}, u32[]{:S(2)}) %all-to-all-start.5) | async-done | bytes 524320 | tf_op jit(solution)/shard_map/all_to_all | solution.py:21
  197.3 1.1 reduce_sum.109
  199.4 1.1 copy.99
  202.9 13.3 %all_to_all.75 = f32[8,32,256]{2,1,0:T(8,128)} all-to-all(f32[8,32,256]{2,1,0:T(8,128)S(1)} %broadcast_in_dim.163), channel_id=1, replica_groups=mesh['grp'=8,'z'=8,'x'=4,'core'=2] {'x','core'}, dimensions={0} | all-to-all | bytes 524288 | tf_op jit(solution)/shard_map/all_to_all | solution.py:21
  217.5 13.9 %all_to_all.76 = f32[8,32,256]{2,1,0:T(8,128)} all-to-all(f32[8,32,256]{2,1,0:T(8,128)S(1)} %broadcast_in_dim.164), channel_id=1, replica_groups=mesh['grp'=8,'z'=8,'x'=4,'core'=2] {'grp'}, dimensions={0} | all-to-all | bytes 524288 | tf_op jit(solution)/shard_map/all_to_all | solution.py:21
  231.4 1.6 reduce_sum.111
  233.9 1.6 slice_subtract_fusion
  235.4 1.0 sub.49
  236.7 12.2 %all_to_all.77 = f32[8,32,256]{2,1,0:T(8,128)} all-to-all(f32[8,32,256]{2,1,0:T(8,128)S(1)} %broadcast_in_dim.165), channel_id=1, replica_groups=mesh['grp'=8,'z'=8,'x'=4,'core'=2] {'x','core'}, dimensions={0} | all-to-all | bytes 524288 | tf_op jit(solution)/shard_map/all_to_all | solution.py:21
  250.1 13.4 %all_to_all.78 = f32[8,32,256]{2,1,0:T(8,128)} all-to-all(f32[8,32,256]{2,1,0:T(8,128)S(1)} %broadcast_in_dim.166), channel_id=1, replica_groups=mesh['grp'=8,'z'=8,'x'=4,'core'=2] {'grp'}, dimensions={0} | all-to-all | bytes 524288 | tf_op jit(solution)/shard_map/all_to_all | solution.py:21
  264.7 11.4 %all_to_all.79 = f32[8,32,256]{2,1,0:T(8,128)S(1)} all-to-all(f32[8,32,256]{2,1,0:T(8,128)S(1)} %broadcast_in_dim.167), channel_id=1, replica_groups=mesh['grp'=8,'z'=8,'x'=4,'core'=2] {'x','core'}, dimensions={0} | all-to-all | bytes 524288 | tf_op jit(solution)/shard_map/all_to_all | solution.py:21
  276.4 12.7 %all_to_all.80 = f32[8,32,256]{2,1,0:T(8,128)S(1)} all-to-all(f32[8,32,256]{2,1,0:T(8,128)S(1)} %broadcast_in_dim.168), channel_id=1, replica_groups=mesh['grp'=8,'z'=8,'x'=4,'core'=2] {'grp'}, dimensions={0} | all-to-all | bytes 524288 | tf_op jit(solution)/shard_map/all_to_all | solution.py:21
  289.3 14.2 %all_to_all.81 = f32[8,32,512]{2,1,0:T(8,128)S(1)} all-to-all(f32[8,32,512]{2,1,0:T(8,128)S(1)} %broadcast_in_dim.169), channel_id=1, replica_groups=mesh['grp'=8,'z'=8,'x'=4,'core'=2] {'x','core'}, dimensions={0} | all-to-all | bytes 1048576 | tf_op jit(solution)/shard_map/all_to_all | solution.py:21
  303.5 1.9 reshape.172
  305.4 4.1 %copy.87 = f32[32,2,8,8,32]{4,3,2,1,0:T(8,128)} copy(f32[32,2,8,8,32]{4,2,1,0,3:T(8,128)} %bitcast.113) | data formatting | bytes 1048576 | tf_op jit(solution)/shard_map/transpose | solution.py:115
  309.5 2.5 reshape.173
  313.2 5.7 %all-to-all-start.13 = ((f32[64,8,128]{2,1,0:T(8,128)}), f32[64,8,128]{2,1,0:T(8,128)S(1)}, u32[]{:S(2)}, u32[]{:S(2)}) async-start(f32[64,8,128]{2,1,0:T(8,128)} %broadcast_in_dim.171), calls=%async_computation.13 | async-start | bytes 524288 | tf_op jit(solution)/shard_map/all_to_all | solution.py:21
  320.2 11.9 %all-to-all-done.13 = f32[64,8,128]{2,1,0:T(8,128)S(1)} async-done(((f32[64,8,128]{2,1,0:T(8,128)}), f32[64,8,128]{2,1,0:T(8,128)S(1)}, u32[]{:S(2)}, u32[]{:S(2)}) %all-to-all-start.13) | async-done | bytes 262176 | tf_op jit(solution)/shard_map/all_to_all | solution.py:21
  332.1 1.4 reshape_reshape.4
  333.5 2.8 copy.89
  336.3 1.5 reshape.175
  337.9 1.0 convolution_bitcast_fusion
  339.6 3.6 %all-to-all-start.14 = ((f32[8,32,256]{2,1,0:T(8,128)}), f32[8,32,256]{2,1,0:T(8,128)S(1)}, u32[]{:S(2)}, u32[]{:S(2)}) async-start(f32[8,32,256]{2,1,0:T(8,128)} %broadcast_in_dim.172), calls=%async_computation.14 | async-start | bytes 524288 | tf_op jit(solution)/shard_map/all_to_all | solution.py:21
  344.1 5.7 %all-to-all-done.14 = f32[8,32,256]{2,1,0:T(8,128)S(1)} async-done(((f32[8,32,256]{2,1,0:T(8,128)}), f32[8,32,256]{2,1,0:T(8,128)S(1)}, u32[]{:S(2)}, u32[]{:S(2)}) %all-to-all-start.14) | async-done | bytes 262176 | tf_op jit(solution)/shard_map/all_to_all | solution.py:21
  (108 shorter events, 22.7 us)
Async XLA Ops:
  0.6 138.6 %copy-start = (f32[32,4096]{1,0:T(8,128)S(1)}, f32[32,4096]{1,0:T(8,128)}, u32[]{:S(2)}) copy-start(f32[32,4096]{1,0:T(8,128)} %param.22) | copy-start | bytes 1572868
  8.6 1.0 copy-start.8
  10.5 11.4 %copy-start.16 = (f32[32,32]{1,0:T(8,128)S(1)}, f32[32,32]{1,0:T(8,128)}, u32[]{:S(2)}) copy-start(f32[32,32]{1,0:T(8,128)} %param.20) | copy-start | bytes 12292
  10.7 24.1 %copy-start.7 = (f32[32,2048]{1,0:T(8,128)S(1)}, f32[32,2048]{1,0:T(8,128)}, u32[]{:S(2)}) copy-start(f32[32,2048]{1,0:T(8,128)} %param.21) | copy-start | bytes 786436
  10.7 24.1 %copy-start.13 = (f32[2,32,256]{2,1,0:T(8,128)S(1)}, f32[2,32,256]{2,1,0:T(8,128)}, u32[]{:S(2)}) copy-start(f32[2,32,256]{2,1,0:T(8,128)} %param.24) | copy-start | bytes 196612
  10.8 24.1 %copy-start.14 = (f32[1,32,256]{2,1,0:T(8,128)S(1)}, f32[1,32,256]{2,1,0:T(8,128)}, u32[]{:S(2)}) copy-start(f32[1,32,256]{2,1,0:T(8,128)} %param.25) | copy-start | bytes 98308
  11.8 16.6 %all-to-all-start = ((f32[8,32,256]{2,1,0:T(8,128)}), f32[8,32,256]{2,1,0:T(8,128)S(1)}, u32[]{:S(2)}, u32[]{:S(2)}) async-start(f32[8,32,256]{2,1,0:T(8,128)} %reshape.163), calls=%async_computation | async-start | bytes 524288 | tf_op jit(solution)/shard_map/all_to_all | solution.py:21
  29.2 15.8 %all-to-all-start.1 = ((f32[8,32,256]{2,1,0:T(8,128)}), f32[8,32,256]{2,1,0:T(8,128)S(1)}, u32[]{:S(2)}, u32[]{:S(2)}) async-start(f32[8,32,256]{2,1,0:T(8,128)} %broadcast_in_dim.159), calls=%async_computation.1 | async-start | bytes 524288 | tf_op jit(solution)/shard_map/all_to_all | solution.py:21
  47.0 69.2 %all-to-all-start.2 = ((f32[8,11,32,256]{3,2,1,0:T(8,128)}), f32[8,11,32,256]{3,2,1,0:T(8,128)}, u32[]{:S(2)}, u32[]{:S(2)}) async-start(f32[8,11,32,256]{3,2,1,0:T(8,128)} %stack.8), calls=%async_computation.2 | async-start | bytes 5767168 | tf_op jit(solution)/shard_map/all_to_all | solution.py:72
  125.1 14.0 %all-to-all-start.3 = ((f32[8,32,256]{2,1,0:T(8,128)}), f32[8,32,256]{2,1,0:T(8,128)S(1)}, u32[]{:S(2)}, u32[]{:S(2)}) async-start(f32[8,32,256]{2,1,0:T(8,128)} %reshape.167), calls=%async_computation.3 | async-start | bytes 524288 | tf_op jit(solution)/shard_map/all_to_all | solution.py:21
  139.2 5.6 %copy-start.10 = (f32[32,256]{1,0:T(8,128)}, f32[32,256]{1,0:T(8,128)S(1)}, u32[]{:S(2)}) copy-start(f32[32,256]{1,0:T(8,128)S(1)} %reduce_sum.107) | copy-start | bytes 98308
  144.8 7.5 %copy-start.15 = (f32[32,2,32]{2,1,0:T(2,128)S(1)}, f32[32,2,32]{2,1,0:T(2,128)}, u32[]{:S(2)}) copy-start(f32[32,2,32]{2,1,0:T(2,128)} %param.23) | copy-start | bytes 24580
  147.2 22.9 %all-to-all-start.4 = ((f32[64,16,128]{2,1,0:T(8,128)}), f32[64,16,128]{2,1,0:T(8,128)S(1)}, u32[]{:S(2)}, u32[]{:S(2)}) async-start(f32[64,16,128]{2,1,0:T(8,128)} %copy.85), calls=%async_computation.4 | async-start | bytes 1048576 | tf_op jit(solution)/shard_map/all_to_all | solution.py:21
  171.1 26.3 %all-to-all-start.5 = ((f32[64,16,128]{2,1,0:T(8,128)}), f32[64,16,128]{2,1,0:T(8,128)}, u32[]{:S(2)}, u32[]{:S(2)}) async-start(f32[64,16,128]{2,1,0:T(8,128)} %broadcast_in_dim.162), calls=%async_computation.5 | async-start | bytes 1048576 | tf_op jit(solution)/shard_map/all_to_all | solution.py:21
  200.5 0.7 copy-start.1
  217.2 14.2 %copy-start.5 = (f32[32,256]{1,0:T(8,128)}, f32[32,256]{1,0:T(8,128)S(1)}, u32[]{:S(2)}) copy-start(f32[32,256]{1,0:T(8,128)S(1)} %reduce_sum.110) | copy-start | bytes 98308
  236.4 39.7 %copy-start.6 = (f32[32,256]{1,0:T(8,128)S(1)}, f32[32,256]{1,0:T(8,128)}, u32[]{:S(2)}) copy-start(f32[32,256]{1,0:T(8,128)} %copy-done.5) | copy-start | bytes 98308
  309.5 2.6 copy-start.11
  313.2 18.8 %all-to-all-start.13 = ((f32[64,8,128]{2,1,0:T(8,128)}), f32[64,8,128]{2,1,0:T(8,128)S(1)}, u32[]{:S(2)}, u32[]{:S(2)}) async-start(f32[64,8,128]{2,1,0:T(8,128)} %broadcast_in_dim.171), calls=%async_computation.13 | async-start | bytes 524288 | tf_op jit(solution)/shard_map/all_to_all | solution.py:21
  339.6 10.1 %all-to-all-start.14 = ((f32[8,32,256]{2,1,0:T(8,128)}), f32[8,32,256]{2,1,0:T(8,128)S(1)}, u32[]{:S(2)}, u32[]{:S(2)}) async-start(f32[8,32,256]{2,1,0:T(8,128)} %broadcast_in_dim.172), calls=%async_computation.14 | async-start | bytes 524288 | tf_op jit(solution)/shard_map/all_to_all | solution.py:21
  344.1 7.1 %copy-start.2 = (f32[2,128,128]{2,1,0:T(8,128)S(1)}, f32[2,128,128]{2,1,0:T(8,128)}, u32[]{:S(2)}) copy-start(f32[2,128,128]{2,1,0:T(8,128)} %param.16) | copy-start | bytes 393220
  344.1 7.1 %copy-start.9 = (f32[32,128]{1,0:T(8,128)S(1)}, f32[32,128]{1,0:T(8,128)}, u32[]{:S(2)}) copy-start(f32[32,128]{1,0:T(8,128)} %copy-done.8) | copy-start | bytes 49156
  344.1 7.2 %copy-start.3 = (f32[2,128,128]{2,1,0:T(8,128)S(1)}, f32[2,128,128]{2,1,0:T(8,128)}, u32[]{:S(2)}) copy-start(f32[2,128,128]{2,1,0:T(8,128)} %param.14) | copy-start | bytes 393220
  350.0 1.7 copy-start.12
  351.2 1.6 copy-start.4
